TPU v7x, 512 devices: a whole 4x4x16 slice. The times are simulated.
512 devices in a mesh: tiles: 128 (over z, y, core), rep: 4 (over x).
Axes of the slice: x: 4, y: 4, z: 16, core: 2. Of those that a mesh axis runs over, the one named last changes fastest.
Arguments:
- tiles: bfloat16 [1024, 64, 4096], P(('tiles', 'rep')), may hold values from -6 to 6
- block_one: int32 [1024], P(('tiles', 'rep')), may hold values from 0 to 127
- block_two: int32 [1024], P(('tiles', 'rep')), may hold values from 0 to 255
- block_three: int32 [1024], P(('tiles', 'rep')), may hold values from 0 to 15
- owner_map: int32 [128], replicated, may hold values from 0 to 127, each once
- u_one: float32 [32, 8192], P(None, 'tiles'), may hold values from -6 to 6
- u_two: bfloat16 [32, 16384], P(None, 'tiles'), may hold values from -6 to 6
- u_three: bfloat16 [32, 1024], replicated, may hold values from -6 to 6
Outputs:
- factor: float32 [32, 8192], P(None, 'tiles')
- tile_factor: bfloat16 [1024, 2048], P(('tiles', 'rep'))
All inputs are finite; a program needn't handle non-finite values.
Results may differ from a plain program's by a relative error of at most 0.0081.
Values may be sent and summed in bfloat16 or wider, within the bound.
A program may use at most 64 MiB of HBM per device.

v0:
```python
import jax
import jax.numpy as jnp
from jax import lax
from jax.sharding import PartitionSpec as P

NS_STEPS = 2


def pick(table, index, width):
    grid = table.reshape(table.shape[0], -1, width)
    return jnp.transpose(jnp.take(grid, index, axis=1), (1, 0, 2))


def gram_total(local):
    return lax.psum(local, "tiles")


def orthonormal(rows, rows_total):
    hi = lax.Precision.HIGHEST
    rank = rows.shape[0]
    g0 = gram_total(jnp.dot(rows, rows.T, precision=hi, preferred_element_type=jnp.float32))
    msq = jnp.trace(g0) / rows_total
    inv = 1.0 / jnp.sqrt(msq + 1e-06)
    x = rows * inv
    g = g0 * (inv * inv) / rows_total
    eye = jnp.eye(rank, dtype=jnp.float32)
    for step in range(NS_STEPS):
        if step > 0:
            g = (
                gram_total(jnp.dot(x, x.T, precision=hi, preferred_element_type=jnp.float32))
                / rows_total
            )
        x = jnp.dot(1.5 * eye - 0.5 * g, x, precision=hi, preferred_element_type=jnp.float32)
    return x


def spread(current):
    cast = current.astype(jnp.bfloat16)
    return lax.all_gather(cast, "tiles", axis=1, tiled=True)


def per_device(tiles, block_one, block_two, block_three, owner_map, u_one, u_two, u_three):
    hi = lax.Precision.HIGHEST
    count = tiles.shape[0]
    width = tiles.shape[1]
    rank = u_three.shape[0]
    blocks_total = owner_map.shape[0]
    rows_total = blocks_total * width
    two_full = lax.all_gather(u_two, "tiles", axis=1, tiled=True)
    two_pick = pick(two_full, block_two, width)
    three_pick = pick(u_three, block_three, width)
    cube = tiles.reshape(count, width, width, width)
    first = jnp.einsum(
        "tijk,tsk->tijs", cube, three_pick, preferred_element_type=jnp.float32
    ).astype(jnp.bfloat16)
    second = jnp.einsum("tijs,trj->tirs", first, two_pick, preferred_element_type=jnp.float32)
    products = second.reshape(count, width, rank * rank).astype(jnp.bfloat16)
    positions = jnp.take(owner_map, block_one)
    onehot = (positions[:, None] == jnp.arange(blocks_total, dtype=jnp.int32)[None, :]).astype(
        jnp.float32
    )
    current = u_one
    readers = pick(spread(current), positions, width)
    partial_value = jnp.einsum("tic,tri->rc", products, readers, preferred_element_type=jnp.float32)
    project = lax.psum(partial_value, ("tiles", "rep")).astype(jnp.bfloat16)
    z_tile = jnp.einsum("rc,tic->tri", project, products, preferred_element_type=jnp.float32)
    term = jnp.einsum("tri,tn->rni", z_tile, onehot, precision=hi).reshape(rank, rows_total)
    rows = lax.psum_scatter(term, "tiles", scatter_dimension=1, tiled=True)
    rows = lax.psum(rows, "rep")
    current = orthonormal(rows, rows_total)
    tile_factor = pick(spread(current), positions, width).reshape(count, rank * width)
    return (current, tile_factor)


def solution(mesh):
    in_specs = (
        P(("tiles", "rep"), None, None),
        P(("tiles", "rep")),
        P(("tiles", "rep")),
        P(("tiles", "rep")),
        P(),
        P(None, "tiles"),
        P(None, "tiles"),
        P(),
    )
    out_specs = (P(None, "tiles"), P(("tiles", "rep"), None))
    return jax.shard_map(
        per_device, mesh=mesh, in_specs=in_specs, out_specs=out_specs, check_vma=False
    )
```

profile of v0, /device:TPU:1, one launch (start us, length us, event | category | flops | bytes accessed | tf_op | source)
XLA Modules:
  0.0 1633.5 jit_solution(5011610970250502089)
XLA Ops:
  7.2 0.0 copy-start
  7.2 0.0 all-gather.4.cloned.1.call-start
  7.2 0.7 all-gather.4.cloned.1.call-update
  7.9 0.0 reduce-scatter.4.cloned.1.call-start
  8.0 0.7 compare_select_fusion.3
  8.6 0.7 convert_bitcast_fusion.1
  9.3 1.0 reshape.51
  10.4 109.1 %all-gather = bf16[128,64,32]{1,2,0:T(8,128)(2,1)S(1)} all-gather(bf16[1,64,32]{1,2,0:T(8,128)(2,1)S(1)} %convert_bitcast_fusion.1), channel_id=1, replica_groups=mesh['tiles'=128,'rep'=4] {'tiles'}, dimensions={0}, use_global_device_ids=true | all-gather | bytes 528384 | tf_op jit(solution)/shard_map/all_gather | solution.py:39
  119.5 0.4 copy.31
  119.9 0.8 reshape.103
  120.7 1.1 reshape.53
  121.9 0.7 copy.32
  122.6 3.4 reshape.52
  126.1 0.6 gather_fusion
  126.7 0.6 gather_fusion.2
  127.3 0.6 gather_fusion.3
  128.0 2.0 fusion
  130.0 17.5 %all-gather.4.cloned.1.call-done = bf16[32,16384]{1,0:T(8,128)(2,1)} async-done(((bf16[32,128]{1,0:T(8,128)(2,1)}), bf16[32,16384]{1,0:T(8,128)(2,1)}) %all-gather.4.cloned.1.call-update) | async-done | bytes 1048592 | tf_op jit(solution)/shard_map/all_gather | solution.py:49
  147.5 3.0 reshape.50
  150.6 2.7 copy.27
  153.3 2.1 gather_fusion.1
  155.4 1.1 fusion.1
  156.5 0.2 copy.30
  156.7 0.2 convolution_bitcast_fusion.1
  157.0 102.8 %all-reduce.1 = bf16[32,1024]{1,0:T(8,128)(2,1)S(1)} all-reduce(f32[32,1024]{1,0:T(8,128)S(1)} %convolution_bitcast_fusion.1), channel_id=1, replica_groups=mesh['tiles'=128,'rep'=4] {'tiles','rep'}, use_global_device_ids=true, to_apply=%region_0.0 | all-reduce | flops 32768 | bytes 196608 | tf_op jit(solution)/shard_map/psum | solution.py:65
  259.7 0.2 convolution_bitcast_fusion.2
  259.9 1.0 convolution_bitcast_fusion
  261.0 4.4 copy.45
  265.4 0.0 reduce-scatter.4.cloned.1.call-update
  265.5 245.9 %reduce-scatter.4.cloned.1.call-done = f32[64,32]{1,0:T(8,128)} async-done(((f32[8192,32]{1,0:T(8,128)}), f32[64,32]{1,0:T(8,128)}) %reduce-scatter.4.cloned.1.call-update) | async-done | bytes 8208
  511.3 0.8 copy.44
  512.2 13.3 psum.29
  525.5 0.1 fusion.44
  525.6 500.6 %psum.30 = f32[32,32]{1,0:T(8,128)S(1)} all-reduce(f32[32,32]{1,0:T(8,128)S(1)} %fusion.44), channel_id=1, replica_groups=mesh['tiles'=128,'rep'=4] {'tiles'}, use_global_device_ids=true, to_apply=%region_3.5 | all-reduce | flops 1024 | bytes 8192 | tf_op jit(solution)/shard_map/psum | solution.py:15
  1026.3 0.6 select_reduce_fusion
  1027.6 0.1 fusion.6
  1027.7 0.2 fusion.45
  1027.9 490.9 %psum.31 = f32[32,32]{1,0:T(8,128)S(1)} all-reduce(f32[32,32]{1,0:T(8,128)S(1)} %fusion.45), channel_id=1, replica_groups=mesh['tiles'=128,'rep'=4] {'tiles'}, use_global_device_ids=true, to_apply=%region_5.7 | all-reduce | flops 1024 | bytes 8192 | tf_op jit(solution)/shard_map/psum | solution.py:15
  1518.7 0.1 fusion.7
  1518.9 0.0 copy-start.1
  1518.9 103.3 %all-gather.1 = bf16[128,64,32]{1,2,0:T(8,128)(2,1)S(1)} all-gather(bf16[1,64,32]{1,2,0:T(8,128)(2,1)S(1)} %convert_bitcast_fusion), channel_id=1, replica_groups=mesh['tiles'=128,'rep'=4] {'tiles'}, dimensions={0}, use_global_device_ids=true | all-gather | bytes 528384 | tf_op jit(solution)/shard_map/all_gather | solution.py:39
  1622.2 0.4 copy.37
  1622.6 0.8 reshape.105
  1623.5 1.1 reshape.55
  1624.6 0.7 copy.38
  1625.3 0.6 gather_fusion.4
  1625.9 0.1 broadcast_select_fusion
  1625.9 0.7 reshape.56
  (20 shorter events, 0.1 us)
Async XLA Ops:
  7.2 118.9 %copy-start = (s32[128]{0:T(128)S(1)}, s32[128]{0:T(128)}, u32[]{:S(2)}) copy-start(s32[128]{0:T(128)} %param.14) | copy-start | bytes 1540
  7.2 140.3 %all-gather.4.cloned.1.call-start = ((), (), s32[]{:S(2)}) async-start(), calls=%async_computation.1 | async-start | bytes 1056768 | tf_op jit(solution)/shard_map/all_gather | solution.py:49
  7.9 503.4 %reduce-scatter.4.cloned.1.call-start = ((), (), s32[]{:S(2)}) async-start(), calls=%async_computation.2 | async-start | bytes 4227072
  122.6 4.2 copy-start.4
  122.6 4.7 copy-start.2
  122.6 5.3 copy-start.3
  1518.9 104.6 %copy-start.1 = (f32[32,64]{1,0:T(8,128)}, f32[32,64]{1,0:T(8,128)S(1)}, u32[]{:S(2)}) copy-start(f32[32,64]{1,0:T(8,128)S(1)} %fusion.7) | copy-start | bytes 24580
Sparse Core Ops, SparseCore 0:
  11.0 136.4 all-gather.3
  265.6 245.7 reduce-scatter.3
where the time goes:
time: 1630 us
  blocking collectives  1320 us (81%)
  waiting for transfers between devices  264 us (16%)
  local copies, waits for them, and re-layouts  27 us (2%)
    psum x2, blocking collectives, gram_total(): return lax.psum(local, 'tiles')  992 us
    unnamed x3, waiting for transfers between devices  247 us
    all_gather x2, blocking collectives, spread(): return lax.all_gather(cast, 'tiles', axis=1, tiled=True)  212 us
    psum x1, blocking collectives, per_device(): project = lax.psum(partial_value, ('tiles', 'rep')).astype(jnp.bfloat16)  103 us
  transfers between devices with their start and end apart: 2, of which 2 were waited for; matrix products, arithmetic and copies ran while one was open for 1% of the time, Pallas kernels for 0%

commit v1 on v0

--- a/solution.py
+++ b/solution.py
@@ -62,7 +62,8 @@
     current = u_one
     readers = pick(spread(current), positions, width)
     partial_value = jnp.einsum("tic,tri->rc", products, readers, preferred_element_type=jnp.float32)
-    project = lax.psum(partial_value, ("tiles", "rep")).astype(jnp.bfloat16)
+    apply_the_sheet = lambda values: lax.psum(lax.psum(values, "tiles"), "rep")
+    project = apply_the_sheet(partial_value).astype(jnp.bfloat16)
     z_tile = jnp.einsum("rc,tic->tri", project, products, preferred_element_type=jnp.float32)
     term = jnp.einsum("tri,tn->rni", z_tile, onehot, precision=hi).reshape(rank, rows_total)
     rows = lax.psum_scatter(term, "tiles", scatter_dimension=1, tiled=True)

time: 1630 us -> 1860 us (1.14)
  waiting for transfers between devices: 264 us -> 581 us
  blocking collectives: 1320 us -> 1230 us
    psum x0 -> x1, waiting for transfers between devices: none -> 313 us  [per_device(): apply_the_sheet = lambda values: lax.psum(lax.psum(values, 'tiles'), 'rep')]
    psum x1, blocking collectives: 103 us -> 15 us  [per_device(): apply_the_sheet = lambda values: lax.psum(lax.psum(values, 'tiles'), 'rep')]
    unnamed x3 -> x4, waiting for transfers between devices: 247 us -> 250 us
  transfers between devices with their start and end apart: 2 -> 3, of which waited for: 2 -> 3; matrix products, arithmetic and copies ran while one was open for 1% -> 1% of each run, Pallas kernels for 0% -> 0%
where the time goes in v1:
time: 1860 us
  blocking collectives  1230 us (66%)
  waiting for transfers between devices  581 us (31%)
  local copies, waits for them, and re-layouts  27 us (1%)
    psum x2, blocking collectives, gram_total(): return lax.psum(local, 'tiles')  992 us
    psum x1, waiting for transfers between devices, per_device(): apply_the_sheet = lambda values: lax.psum(lax.psum(values, 'tiles'), 'rep')  313 us
    unnamed x4, waiting for transfers between devices  250 us
    all_gather x2, blocking collectives, spread(): return lax.all_gather(cast, 'tiles', axis=1, tiled=True)  212 us
  transfers between devices with their start and end apart: 3, of which 3 were waited for; matrix products, arithmetic and copies ran while one was open for 1% of the time, Pallas kernels for 0%

profile of v1, /device:TPU:1, one launch (start us, length us, event | category | flops | bytes accessed | tf_op | source)
XLA Modules:
  0.0 1862.7 jit_solution(9982444385891303892)
XLA Ops:
  7.2 0.0 all-gather.4.cloned.1.call-start
  7.2 0.7 all-gather.4.cloned.1.call-update
  7.9 0.0 all-reduce.3.cloned.1.call-start
  8.0 0.7 compare_select_fusion.3
  8.6 0.7 convert_bitcast_fusion.1
  9.3 1.0 reshape.51
  10.4 109.1 %all-gather = bf16[128,64,32]{1,2,0:T(8,128)(2,1)S(1)} all-gather(bf16[1,64,32]{1,2,0:T(8,128)(2,1)S(1)} %convert_bitcast_fusion.1), channel_id=1, replica_groups=mesh['tiles'=128,'rep'=4] {'tiles'}, dimensions={0}, use_global_device_ids=true | all-gather | bytes 528384 | tf_op jit(solution)/shard_map/all_gather | solution.py:39
  119.5 0.4 copy.31
  119.9 0.8 reshape.103
  120.7 1.1 reshape.53
  121.9 0.7 copy.32
  122.6 3.4 reshape.52
  126.1 0.6 gather_fusion
  126.7 0.6 gather_fusion.2
  127.3 0.6 gather_fusion.3
  128.0 2.0 fusion
  130.0 17.5 all-gather.4.cloned.1.call-done
  147.5 3.0 reshape.50
  150.6 2.7 copy.27
  153.3 2.1 gather_fusion.1
  155.4 1.1 fusion.1
  156.5 0.2 copy.30
  156.7 0.9 convolution_bitcast_fusion.1
  157.6 0.0 all-reduce.3.cloned.1.call-update
  157.7 0.0 reduce-scatter.4.cloned.1.call-start
  157.7 313.3 %all-reduce.3.cloned.1.call-done = f32[32,1024]{1,0:T(8,128)} async-done(((f32[32,1024]{1,0:T(8,128)}), f32[32,1024]{1,0:T(8,128)}) %all-reduce.3.cloned.1.call-update) | async-done | bytes 131088 | tf_op jit(solution)/shard_map/psum | solution.py:65
  471.0 15.0 all-reduce.4
  486.0 0.2 convolution_bitcast_fusion.2
  486.2 1.0 convolution_bitcast_fusion
  487.3 4.4 copy.45
  491.8 249.0 %reduce-scatter.4.cloned.1.call-done = f32[64,32]{1,0:T(8,128)} async-done(((f32[8192,32]{1,0:T(8,128)}), f32[64,32]{1,0:T(8,128)}) %reduce-scatter.4.cloned.1.call-update) | async-done | bytes 8208
  740.8 0.8 copy.44
  741.6 13.4 psum.37
  755.0 0.1 fusion.44
  755.2 500.6 %psum.38 = f32[32,32]{1,0:T(8,128)S(1)} all-reduce(f32[32,32]{1,0:T(8,128)S(1)} %fusion.44), channel_id=1, replica_groups=mesh['tiles'=128,'rep'=4] {'tiles'}, use_global_device_ids=true, to_apply=%region_4.6 | all-reduce | flops 1024 | bytes 8192 | tf_op jit(solution)/shard_map/psum | solution.py:15
  1255.8 0.6 select_reduce_fusion
  1257.1 0.1 fusion.6
  1257.2 0.2 fusion.45
  1257.4 490.9 %psum.39 = f32[32,32]{1,0:T(8,128)S(1)} all-reduce(f32[32,32]{1,0:T(8,128)S(1)} %fusion.45), channel_id=1, replica_groups=mesh['tiles'=128,'rep'=4] {'tiles'}, use_global_device_ids=true, to_apply=%region_6.8 | all-reduce | flops 1024 | bytes 8192 | tf_op jit(solution)/shard_map/psum | solution.py:15
  1748.3 0.1 fusion.7
  1748.4 103.3 %all-gather.1 = bf16[128,64,32]{1,2,0:T(8,128)(2,1)S(1)} all-gather(bf16[1,64,32]{1,2,0:T(8,128)(2,1)S(1)} %convert_bitcast_fusion), channel_id=1, replica_groups=mesh['tiles'=128,'rep'=4] {'tiles'}, dimensions={0}, use_global_device_ids=true | all-gather | bytes 528384 | tf_op jit(solution)/shard_map/all_gather | solution.py:39
  1851.7 0.4 copy.37
  1852.1 0.8 reshape.105
  1853.0 1.1 reshape.55
  1854.1 0.7 copy.38
  1854.8 0.6 gather_fusion.4
  1855.4 0.1 broadcast_select_fusion
  1855.4 0.7 reshape.56
  (23 shorter events, 0.2 us)
Async XLA Ops:
  7.2 118.9 %copy-start = (s32[128]{0:T(128)S(1)}, s32[128]{0:T(128)}, u32[]{:S(2)}) copy-start(s32[128]{0:T(128)} %param.14) | copy-start | bytes 1540
  7.2 140.3 %all-gather.4.cloned.1.call-start = ((), (), s32[]{:S(2)}) async-start(), calls=%async_computation.1 | async-start | bytes 1056768 | tf_op jit(solution)/shard_map/all_gather | solution.py:49
  7.9 463.1 %all-reduce.3.cloned.1.call-start = ((), (), s32[]{:S(2)}) async-start(), calls=%async_computation.2 | async-start | bytes 262144 | tf_op jit(solution)/shard_map/psum | solution.py:65
  122.6 4.2 copy-start.4
  122.6 4.7 copy-start.2
  122.6 5.3 copy-start.3
  157.7 583.1 %reduce-scatter.4.cloned.1.call-start = ((), (), s32[]{:S(2)}) async-start(), calls=%async_computation.3 | async-start | bytes 4227072
  1748.4 104.6 %copy-start.1 = (f32[32,64]{1,0:T(8,128)}, f32[32,64]{1,0:T(8,128)S(1)}, u32[]{:S(2)}) copy-start(f32[32,64]{1,0:T(8,128)S(1)} %fusion.7) | copy-start | bytes 24580
Sparse Core Ops, SparseCore 0:
  11.0 136.4 all-gather.3
  157.8 313.1 all-reduce.2
  491.9 248.8 reduce-scatter.3
